TPU v7x, 256 devices: a whole 4x4x8 slice. The times are simulated.
256 devices in a mesh: seq: 16 (over x_lo, z), tp: 16 (over x_hi, y, core).
Axes of the slice: x: 4 (x_hi: 2, x_lo: 2; x = x_hi * 2 + x_lo), y: 4, z: 8, core: 2. Of those that a mesh axis runs over, the one named last changes fastest.
Arguments:
- tokens: bfloat16 [8192, 2048], P('seq', 'tp'), may hold values from -6 to 6
- w_first: bfloat16 [16, 512, 512], P('seq'), may hold values from -0.25 to 0.25
- second_factor_weight: bfloat16 [512, 16, 16], P('seq'), may hold values from -1.5 to 1.5
- w_up: bfloat16 [64, 2, 128, 128], P('tp'), may hold values from -0.375 to 0.375
- w_self: bfloat16 [6, 64, 128, 128], P(None, 'tp'), may hold values from -0.375 to 0.375
- w_cross: bfloat16 [6, 64, 128, 128], P(None, 'tp'), may hold values from -0.375 to 0.375
- w_down: bfloat16 [64, 2, 128, 128], P('tp'), may hold values from -0.1875 to 0.1875
- block_pairs: int32 [64, 2], P('tp'), may hold values from 0 to 15, all different within a row
- cotangent: bfloat16 [8192, 2048], P('seq', 'tp'), may hold values from -6 to 6
Outputs:
- layer_out: bfloat16 [8192, 2048], P('seq', 'tp')
- grad_tokens: bfloat16 [8192, 2048], P('seq', 'tp')
- grad_first: float32 [16, 512, 512], P('seq')
- gradient_second_factor: float32 [512, 16, 16], P('seq')
- grad_self: float32 [6, 64, 128, 128], P(None, 'tp', 'seq')
- grad_cross: float32 [6, 64, 128, 128], P(None, 'tp', 'seq')
Inputs may be any that keep to these rules, and one draw needn't show every extreme that they name: `block_pairs`: each row names two different input blocks, and every one of the 16 input blocks is named by some row.
All inputs are finite; a program needn't handle non-finite values.
Results may differ from a plain program's by a relative error of at most 0.019.
Values may be sent and summed in bfloat16 or wider, within the bound.
No kernel may reach another device: no remote copies, remote signals or barrier semaphores. Data moves between devices by JAX's collectives and lax.ppermute only.
A program may use at most 64 MiB of HBM per device.

v0:
```python
import math
import jax
import jax.numpy as jnp
from jax import lax
from jax.sharding import PartitionSpec as P


def partner_2(value, axis, bit):
    mask = 2**bit
    pairs = [(source, source ^ mask) for source in range(lax.axis_size(axis))]
    return lax.ppermute(value, axis, pairs)


def gelu_tanh(value):
    return jax.nn.gelu(value, approximate=True)


def swap_local(state, level):
    span = 2**level
    shape = state.shape
    folded = state.reshape(shape[0], shape[1] // (2 * span), 2, span, shape[2])
    return jnp.flip(folded, axis=2).reshape(shape)


def apply_blocks(state, weight):
    return jnp.einsum("rjc,jce->rje", state, weight, preferred_element_type=jnp.float32)


def apply_transposed(state, weight):
    return jnp.einsum("rje,jce->rjc", state, weight, preferred_element_type=jnp.float32)


def outer_blocks(left, right):
    return jnp.einsum("rjc,rje->jce", left, right, preferred_element_type=jnp.float32)


def per_device(
    tokens, w_first, second_factor_weight, w_up, w_self, w_cross, w_down, block_pairs, cotangent
):
    seq_len, width_local = tokens.shape
    group_count, block_len, _ = w_first.shape
    levels = w_self.shape[0]
    slots = w_self.shape[1]
    block_width = w_self.shape[2]
    model_width = width_local * lax.axis_size("tp")
    in_blocks = model_width // block_width
    local_bits = slots.bit_length() - 1
    total_tokens = seq_len * lax.axis_size("seq")
    token_scale = 1.0 / math.sqrt(total_tokens)
    model_width_scale = 1.0 / math.sqrt(model_width)
    grouped = tokens.reshape(group_count, block_len, width_local)
    first_factor_output = jnp.einsum(
        "acb,abd->acd", w_first, grouped, preferred_element_type=jnp.float32
    ).astype(jnp.bfloat16)
    received_rows = lax.all_to_all(
        first_factor_output, "seq", split_axis=1, concat_axis=0, tiled=True
    )
    mixed_part = jnp.einsum(
        "vyi,ivz->yvz", second_factor_weight, received_rows, preferred_element_type=jnp.float32
    ).astype(jnp.bfloat16)
    returned = lax.all_to_all(mixed_part, "seq", split_axis=0, concat_axis=1, tiled=True)
    mixed_tokens = returned
    first_factor_shifted = received_rows
    hidden_in = (
        tokens.astype(jnp.float32) + mixed_tokens.reshape(seq_len, width_local).astype(jnp.float32)
    ).astype(jnp.bfloat16)
    hidden_all, cotangent_all = (
        lax.all_gather(hidden_in, "tp", axis=1, tiled=True),
        lax.all_gather(cotangent, "tp", axis=1, tiled=True),
    )
    flat_pairs = block_pairs.reshape(-1)
    chosen = (
        block_pairs[:, :, None] == jnp.arange(in_blocks, dtype=jnp.int32)[None, None, :]
    ).astype(jnp.float32)
    picked = jnp.take(
        hidden_all.reshape(seq_len, in_blocks, block_width), flat_pairs, axis=1
    ).reshape(seq_len, slots, 2, block_width)
    state = jnp.einsum("rjkc,jkce->rje", picked, w_up, preferred_element_type=jnp.float32).astype(
        jnp.bfloat16
    )
    states = [state]
    partners = [None] * levels
    for level_at in range(levels):
        if level_at < local_bits:
            partner = swap_local(state, level_at)
        else:
            partner = partner_2(state, "tp", level_at - local_bits)
        partners[level_at] = partner
        state = (
            apply_blocks(state, w_self[level_at]) + apply_blocks(partner, w_cross[level_at])
        ).astype(jnp.bfloat16)
        states.append(state)
    top = state.astype(jnp.float32)
    activated = gelu_tanh(top).astype(jnp.bfloat16)
    pieces = jnp.einsum("rjc,jkce->rjke", activated, w_down, preferred_element_type=jnp.float32)
    down_term = jnp.einsum(
        "rjke,jki->rie", pieces, chosen, precision=lax.Precision.HIGHEST
    ).reshape(seq_len, model_width)
    down_part = lax.psum_scatter(down_term, "tp", scatter_dimension=1, tiled=True)
    layer_out = (hidden_in.astype(jnp.float32) + down_part).astype(jnp.bfloat16)
    grad_picked = jnp.take(
        cotangent_all.reshape(seq_len, in_blocks, block_width), flat_pairs, axis=1
    ).reshape(seq_len, slots, 2, block_width)
    grad_act = jnp.einsum("rjke,jkce->rjc", grad_picked, w_down, preferred_element_type=jnp.float32)
    _, pull = jax.vjp(gelu_tanh, top)
    grad_state = pull(grad_act)[0].astype(jnp.bfloat16)
    self_terms = [None] * levels
    cross_terms = [None] * levels
    for level_at in reversed(range(levels)):
        below = states[level_at]
        self_terms[level_at] = outer_blocks(below, grad_state)
        swap_bit = level_at - local_bits
        if level_at < local_bits:
            cross_terms[level_at] = outer_blocks(partners[level_at], grad_state)
            incoming = swap_local(apply_transposed(grad_state, w_cross[level_at]), level_at)
        else:
            cross_terms[level_at] = outer_blocks(partners[level_at], grad_state)
            incoming = partner_2(apply_transposed(grad_state, w_cross[level_at]), "tp", swap_bit)
        grad_state = (apply_transposed(grad_state, w_self[level_at]) + incoming).astype(
            jnp.bfloat16
        )
    back_pieces = jnp.einsum("rje,jkce->rjkc", grad_state, w_up, preferred_element_type=jnp.float32)
    spread = jnp.einsum(
        "rjkc,jki->ric", back_pieces, chosen, precision=lax.Precision.HIGHEST
    ).reshape(seq_len, model_width)
    spread_part = lax.psum_scatter(spread, "tp", scatter_dimension=1, tiled=True)
    grad_hidden = (cotangent.astype(jnp.float32) + spread_part).astype(jnp.bfloat16)
    level_self, level_cross = (
        lax.psum_scatter(jnp.stack(self_terms), "seq", scatter_dimension=2, tiled=True),
        lax.psum_scatter(jnp.stack(cross_terms), "seq", scatter_dimension=2, tiled=True),
    )
    received_rows = lax.all_to_all(
        grad_hidden.reshape(group_count, block_len, width_local),
        "seq",
        split_axis=1,
        concat_axis=0,
        tiled=True,
    )
    moved_back = jnp.einsum(
        "emj,meg->jeg", second_factor_weight, received_rows, preferred_element_type=jnp.float32
    ).astype(jnp.bfloat16)
    returned = lax.all_to_all(moved_back, "seq", split_axis=0, concat_axis=1, tiled=True)
    second_part = jnp.einsum(
        "tfm,lfm->ftl", received_rows, first_factor_shifted, preferred_element_type=jnp.float32
    )
    first_part = jnp.einsum("acd,abd->acb", returned, grouped, preferred_element_type=jnp.float32)
    second_sum, first_sum = lax.psum((second_part, first_part), "tp")
    grad_mix = jnp.einsum(
        "acb,acd->abd", w_first, returned, preferred_element_type=jnp.float32
    ).reshape(seq_len, width_local)
    grad_tokens = (grad_hidden.astype(jnp.float32) + grad_mix).astype(jnp.bfloat16)
    return (
        layer_out,
        grad_tokens,
        first_sum * model_width_scale,
        second_sum * model_width_scale,
        level_self * token_scale,
        level_cross * token_scale,
    )


def solution(mesh):
    in_specs = (
        P("seq", "tp"),
        P("seq", None, None),
        P("seq", None, None),
        P("tp", None, None, None),
        P(None, "tp", None, None),
        P(None, "tp", None, None),
        P("tp", None, None, None),
        P("tp", None),
        P("seq", "tp"),
    )
    out_specs = (
        P("seq", "tp"),
        P("seq", "tp"),
        P("seq", None, None),
        P("seq", None, None),
        P(None, "tp", "seq", None),
        P(None, "tp", "seq", None),
    )
    return jax.shard_map(
        per_device, mesh=mesh, in_specs=in_specs, out_specs=out_specs, check_vma=False
    )
```

profile of v0, /device:TPU:1, one launch (start us, length us, event | category | flops | bytes accessed | tf_op | source)
XLA Modules:
  0.0 764.0 jit_solution(14847866580858052665)
XLA Ops:
  13.0 10.0 %all-to-all-start = ((bf16[16,2,2048]{2,1,0:T(2,128)(2,1)}), bf16[16,2,2048]{2,1,0:T(2,128)(2,1)S(1)}, u32[]{:S(2)}, u32[]{:S(2)}) async-start(bf16[16,2,2048]{2,1,0:T(2,128)(2,1)} %reshape.151), calls=%async_computation | async-start | bytes 262144 | tf_op jit(solution)/shard_map/all_to_all | solution.py:55
  23.3 7.3 all-to-all-done
  31.0 10.6 %all_to_all.42 = bf16[16,32,128]{2,1,0:T(8,128)(2,1)S(1)} all-to-all(bf16[16,32,128]{2,1,0:T(8,128)(2,1)S(1)} %copy.138), channel_id=1, replica_groups=mesh['seq'=16,'tp'=16] {'seq'}, dimensions={0} | all-to-all | bytes 262144 | tf_op jit(solution)/shard_map/all_to_all | solution.py:61
  42.6 25.5 %all-gather.5.cloned.1.call-done = bf16[512,2048]{0,1:T(8,128)(2,1)} async-done(((bf16[512,128]{0,1:T(8,128)(2,1)}), bf16[512,2048]{0,1:T(8,128)(2,1)}) %all-gather.5.cloned.1.call-update) | async-done | bytes 2097168 | tf_op jit(solution)/shard_map/all_gather | solution.py:69
  72.8 49.2 %all-gather.3.cloned.1.call-done = bf16[512,2048]{1,0:T(8,128)(2,1)} async-done(((bf16[512,128]{1,0:T(8,128)(2,1)}), bf16[512,2048]{1,0:T(8,128)(2,1)}) %all-gather.3.cloned.1.call-update) | async-done | bytes 2097168 | tf_op jit(solution)/shard_map/all_gather | solution.py:68
  139.7 12.8 %collective-permute-done.1 = bf16[512,4,128]{2,0,1:T(8,128)(2,1)S(1)} collective-permute-done((bf16[512,4,128]{2,0,1:T(8,128)(2,1)S(1)}, bf16[512,4,128]{2,0,1:T(8,128)(2,1)S(1)}, u32[]{:S(2)}, u32[]{:S(2)}) %collective-permute-start.1) | collective-permute-done | bytes 524320 | tf_op jit(solution)/shard_map/ppermute | solution.py:11
  154.4 12.5 %collective-permute-done.2 = bf16[512,4,128]{2,0,1:T(8,128)(2,1)S(1)} collective-permute-done((bf16[512,4,128]{2,0,1:T(8,128)(2,1)S(1)}, bf16[512,4,128]{2,0,1:T(8,128)(2,1)S(1)}, u32[]{:S(2)}, u32[]{:S(2)}) %collective-permute-start.2) | collective-permute-done | bytes 524320 | tf_op jit(solution)/shard_map/ppermute | solution.py:11
  167.8 12.5 %collective-permute-done.3 = bf16[512,4,128]{2,0,1:T(8,128)(2,1)S(1)} collective-permute-done((bf16[512,4,128]{2,0,1:T(8,128)(2,1)S(1)}, bf16[512,4,128]{2,0,1:T(8,128)(2,1)S(1)}, u32[]{:S(2)}, u32[]{:S(2)}) %collective-permute-start.3) | collective-permute-done | bytes 524320 | tf_op jit(solution)/shard_map/ppermute | solution.py:11
  182.2 23.2 %collective-permute-done.4 = f32[512,4,128]{2,0,1:T(8,128)S(1)} collective-permute-done((f32[512,4,128]{2,0,1:T(8,128)S(1)}, f32[512,4,128]{2,0,1:T(8,128)S(1)}, u32[]{:S(2)}, u32[]{:S(2)}) %collective-permute-start.4) | collective-permute-done | bytes 1048608 | tf_op jit(solution)/shard_map/ppermute | solution.py:11
  207.3 21.5 %collective-permute-done.5 = f32[512,4,128]{2,0,1:T(8,128)S(1)} collective-permute-done((f32[512,4,128]{2,0,1:T(8,128)S(1)}, f32[512,4,128]{2,0,1:T(8,128)S(1)}, u32[]{:S(2)}, u32[]{:S(2)}) %collective-permute-start.5) | collective-permute-done | bytes 1048608 | tf_op jit(solution)/shard_map/ppermute | solution.py:11
  230.1 19.1 %collective-permute-done.6 = f32[512,4,128]{2,0,1:T(8,128)S(1)} collective-permute-done((f32[512,4,128]{2,0,1:T(8,128)S(1)}, f32[512,4,128]{2,0,1:T(8,128)S(1)}, u32[]{:S(2)}, u32[]{:S(2)}) %collective-permute-start.6) | collective-permute-done | bytes 1048608 | tf_op jit(solution)/shard_map/ppermute | solution.py:11
  249.8 6.0 collective-permute-start.7
  271.2 7.2 convolution_bitcast_fusion
  278.5 5.4 copy.192
  285.6 4.1 fusion.1
  289.7 4.0 copy.210
  309.2 59.9 %reduce-scatter.7.cloned.1.call-done = f32[512,128]{0,1:T(8,128)} async-done(((f32[512,2048]{0,1:T(8,128)}), f32[512,128]{0,1:T(8,128)}) %reduce-scatter.7.cloned.1.call-update) | async-done | bytes 262160 | tf_op jit(solution)/shard_map/reduce_scatter | solution.py:126
  371.8 14.1 %all_to_all.43 = bf16[16,2,2048]{2,1,0:T(2,128)(2,1)S(1)} all-to-all(bf16[16,2,2048]{2,1,0:T(2,128)(2,1)S(1)} %reshape.153), channel_id=1, replica_groups=mesh['seq'=16,'tp'=16] {'seq'}, dimensions={0} | all-to-all | bytes 262144 | tf_op jit(solution)/shard_map/all_to_all | solution.py:132
  386.9 3.5 all-to-all-start.3
  390.5 70.1 %reduce-scatter.5.cloned.1.call-done = f32[512,128]{1,0:T(8,128)} async-done(((f32[512,2048]{1,0:T(8,128)}), f32[512,128]{1,0:T(8,128)}) %reduce-scatter.5.cloned.1.call-update) | async-done | bytes 262160 | tf_op jit(solution)/shard_map/reduce_scatter | solution.py:99
  463.6 62.4 %reduce-scatter.11.cloned.1.call-done = f32[6,4,8,128]{3,2,1,0:T(8,128)} async-done(((f32[6,4,128,128]{3,2,1,0:T(8,128)}), f32[6,4,8,128]{3,2,1,0:T(8,128)}) %reduce-scatter.11.cloned.1.call-update) | async-done | bytes 98320 | tf_op jit(solution)/shard_map/reduce_scatter | solution.py:130
  527.5 70.6 %reduce-scatter.9.cloned.1.call-done = f32[6,4,8,128]{3,2,1,0:T(8,128)} async-done(((f32[6,4,128,128]{3,2,1,0:T(8,128)}), f32[6,4,8,128]{3,2,1,0:T(8,128)}) %reduce-scatter.9.cloned.1.call-update) | async-done | bytes 98320 | tf_op jit(solution)/shard_map/reduce_scatter | solution.py:129
  599.8 73.2 %psum.15 = f32[32,16,16]{2,1,0:T(8,128)S(1)} all-reduce(f32[32,16,16]{2,1,0:T(8,128)S(1)} %fusion.97), channel_id=1, replica_groups=mesh['seq'=16,'tp'=16] {'tp'}, use_global_device_ids=true, to_apply=%region_3.5 | all-reduce | flops 8192 | bytes 65536 | tf_op jit(solution)/shard_map/psum | solution.py:147
  674.9 80.0 %all-reduce.2.cloned.1.call-done = f32[1,512,512]{2,1,0:T(8,128)} async-done(((f32[1,512,512]{2,1,0:T(8,128)}), f32[1,512,512]{2,1,0:T(8,128)}) %all-reduce.2.cloned.1.call-update) | async-done | bytes 1048592 | tf_op jit(solution)/shard_map/psum | solution.py:147
  (186 shorter events, 84.5 us)
Async XLA Ops:
  7.2 16.0 %copy-start.37 = (bf16[32,16,16]{0,2,1:T(8,128)(2,1)S(1)}, bf16[32,16,16]{0,2,1:T(8,128)(2,1)}, u32[]{:S(2)}) copy-start(bf16[32,16,16]{0,2,1:T(8,128)(2,1)} %param.13) | copy-start | bytes 49156
  7.2 60.9 %all-gather.5.cloned.1.call-start = ((), (), s32[]{:S(2)}) async-start(), calls=%async_computation.10 | async-start | bytes 2228224 | tf_op jit(solution)/shard_map/all_gather | solution.py:69
  10.2 31.4 %copy-start.31 = (bf16[512,128]{1,0:T(8,128)(2,1)S(1)}, bf16[512,128]{1,0:T(8,128)(2,1)}, u32[]{:S(2)}) copy-start(bf16[512,128]{1,0:T(8,128)(2,1)} %param.11) | copy-start | bytes 393220
  12.3 30.1 %copy-start.38 = (s32[4,2]{0,1:T(2,128)S(1)}, s32[4,2]{0,1:T(2,128)}, u32[]{:S(2)}) copy-start(s32[4,2]{0,1:T(2,128)} %param.18) | copy-start | bytes 100
  13.0 17.6 %all-to-all-start = ((bf16[16,2,2048]{2,1,0:T(2,128)(2,1)}), bf16[16,2,2048]{2,1,0:T(2,128)(2,1)S(1)}, u32[]{:S(2)}, u32[]{:S(2)}) async-start(bf16[16,2,2048]{2,1,0:T(2,128)(2,1)} %reshape.151), calls=%async_computation | async-start | bytes 262144 | tf_op jit(solution)/shard_map/all_to_all | solution.py:55
  23.1 98.9 %all-gather.3.cloned.1.call-start = ((), (), s32[]{:S(2)}) async-start(), calls=%async_computation.8 | async-start | bytes 2228224 | tf_op jit(solution)/shard_map/all_gather | solution.py:68
  42.4 326.8 %reduce-scatter.7.cloned.1.call-start = ((), (), s32[]{:S(2)}) async-start(), calls=%async_computation.11 | async-start | bytes 4456448 | tf_op jit(solution)/shard_map/reduce_scatter | solution.py:126
  136.9 2.0 collective-permute-start
  139.3 13.3 %collective-permute-start.1 = (bf16[512,4,128]{2,0,1:T(8,128)(2,1)S(1)}, bf16[512,4,128]{2,0,1:T(8,128)(2,1)S(1)}, u32[]{:S(2)}, u32[]{:S(2)}) collective-permute-start(bf16[512,4,128]{2,0,1:T(8,128)(2,1)S(1)} %fusion.27), channel_id=1, source_target_pairs={{0,2},{1,3},{2,0},{3,1},{4,6},{5,7},{6,4},{7,5},{8,10},{9,11},{10,... | collective-permute-start | bytes 1572872 | tf_op jit(solution)/shard_map/ppermute | solution.py:11
  152.9 14.0 %collective-permute-start.2 = (bf16[512,4,128]{2,0,1:T(8,128)(2,1)S(1)}, bf16[512,4,128]{2,0,1:T(8,128)(2,1)S(1)}, u32[]{:S(2)}, u32[]{:S(2)}) collective-permute-start(bf16[512,4,128]{2,0,1:T(8,128)(2,1)S(1)} %fusion.26), channel_id=1, source_target_pairs={{0,4},{1,5},{2,6},{3,7},{4,0},{5,1},{6,2},{7,3},{8,12},{9,13},{10,... | collective-permute-start | bytes 1572872 | tf_op jit(solution)/shard_map/ppermute | solution.py:11
  167.2 13.1 %collective-permute-start.3 = (bf16[512,4,128]{2,0,1:T(8,128)(2,1)S(1)}, bf16[512,4,128]{2,0,1:T(8,128)(2,1)S(1)}, u32[]{:S(2)}, u32[]{:S(2)}) collective-permute-start(bf16[512,4,128]{2,0,1:T(8,128)(2,1)S(1)} %fusion.25), channel_id=1, source_target_pairs={{0,8},{1,9},{2,10},{3,11},{4,12},{5,13},{6,14},{7,15},{8,0},{9,1},... | collective-permute-start | bytes 1572872 | tf_op jit(solution)/shard_map/ppermute | solution.py:11
  181.6 24.1 %copy-start.4 = (bf16[512,4,128]{2,0,1:T(8,128)(2,1)}, bf16[512,4,128]{2,0,1:T(8,128)(2,1)S(1)}, u32[]{:S(2)}) copy-start(bf16[512,4,128]{2,0,1:T(8,128)(2,1)S(1)} %fusion.52) | copy-start | bytes 1572868
  181.9 23.5 %collective-permute-start.4 = (f32[512,4,128]{2,0,1:T(8,128)S(1)}, f32[512,4,128]{2,0,1:T(8,128)S(1)}, u32[]{:S(2)}, u32[]{:S(2)}) collective-permute-start(f32[512,4,128]{2,0,1:T(8,128)S(1)} %convolution_bitcast_fusion.12), channel_id=1, source_target_pairs={{0,8},{1,9},{2,10},{3,11},{4,12},{5,13},{6,14},{7,15},{8,0},{9,1},... | collective-permute-start | bytes 3145736 | tf_op jit(solution)/shard_map/ppermute | solution.py:11
  206.0 22.8 %collective-permute-start.5 = (f32[512,4,128]{2,0,1:T(8,128)S(1)}, f32[512,4,128]{2,0,1:T(8,128)S(1)}, u32[]{:S(2)}, u32[]{:S(2)}) collective-permute-start(f32[512,4,128]{2,0,1:T(8,128)S(1)} %convolution_bitcast_fusion.10), channel_id=1, source_target_pairs={{0,4},{1,5},{2,6},{3,7},{4,0},{5,1},{6,2},{7,3},{8,12},{9,13},{10,... | collective-permute-start | bytes 3145736 | tf_op jit(solution)/shard_map/ppermute | solution.py:11
  229.4 19.7 %collective-permute-start.6 = (f32[512,4,128]{2,0,1:T(8,128)S(1)}, f32[512,4,128]{2,0,1:T(8,128)S(1)}, u32[]{:S(2)}, u32[]{:S(2)}) collective-permute-start(f32[512,4,128]{2,0,1:T(8,128)S(1)} %convolution_bitcast_fusion.8), channel_id=1, source_target_pairs={{0,2},{1,3},{2,0},{3,1},{4,6},{5,7},{6,4},{7,5},{8,10},{9,11},{10,... | collective-permute-start | bytes 3145736 | tf_op jit(solution)/shard_map/ppermute | solution.py:11
  249.8 8.3 %collective-permute-start.7 = (f32[512,4,128]{2,0,1:T(8,128)S(1)}, f32[512,4,128]{2,0,1:T(8,128)S(1)}, u32[]{:S(2)}, u32[]{:S(2)}) collective-permute-start(f32[512,4,128]{2,0,1:T(8,128)S(1)} %convolution_bitcast_fusion.6), channel_id=1, source_target_pairs={{0,1},{1,0},{2,3},{3,2},{4,5},{5,4},{6,7},{7,6},{8,9},{9,8},{10,11... | collective-permute-start | bytes 3145736 | tf_op jit(solution)/shard_map/ppermute | solution.py:11
  283.8 176.8 %reduce-scatter.5.cloned.1.call-start = ((), (), s32[]{:S(2)}) async-start(), calls=%async_computation.9 | async-start | bytes 4456448 | tf_op jit(solution)/shard_map/reduce_scatter | solution.py:99
  293.8 232.2 %reduce-scatter.11.cloned.1.call-start = ((), (), s32[]{:S(2)}) async-start(), calls=%async_computation.14 | async-start | bytes 1671168 | tf_op jit(solution)/shard_map/reduce_scatter | solution.py:130
  301.6 296.5 %reduce-scatter.9.cloned.1.call-start = ((), (), s32[]{:S(2)}) async-start(), calls=%async_computation.13 | async-start | bytes 1671168 | tf_op jit(solution)/shard_map/reduce_scatter | solution.py:129
  308.2 61.0 %copy-start.28 = (bf16[512,128]{0,1:T(8,128)(2,1)S(1)}, bf16[512,128]{0,1:T(8,128)(2,1)}, u32[]{:S(2)}) copy-start(bf16[512,128]{0,1:T(8,128)(2,1)} %copy.147) | copy-start | bytes 393220
  370.1 90.5 %copy-start.32 = (bf16[512,128]{1,0:T(8,128)(2,1)S(1)}, bf16[512,128]{1,0:T(8,128)(2,1)}, u32[]{:S(2)}) copy-start(bf16[512,128]{1,0:T(8,128)(2,1)} %fusion.65) | copy-start | bytes 393220
  386.9 75.3 %all-to-all-start.3 = ((bf16[16,32,128]{2,1,0:T(8,128)(2,1)}), bf16[16,32,128]{2,1,0:T(8,128)(2,1)S(1)}, u32[]{:S(2)}, u32[]{:S(2)}) async-start(bf16[16,32,128]{2,1,0:T(8,128)(2,1)} %copy.155), calls=%async_computation.5 | async-start | bytes 262144 | tf_op jit(solution)/shard_map/all_to_all | solution.py:142
  390.5 364.4 %all-reduce.2.cloned.1.call-start = ((), (), s32[]{:S(2)}) async-start(), calls=%async_computation.12 | async-start | bytes 2097152 | tf_op jit(solution)/shard_map/psum | solution.py:147
  463.5 210.3 %copy-start.35 = (f32[512,128]{0,1:T(8,128)S(1)}, f32[512,128]{0,1:T(8,128)}, u32[]{:S(2)}) copy-start(f32[512,128]{0,1:T(8,128)} %reduce-scatter.7.cloned.1.call-done) | copy-start | bytes 786436
  (32 other events, 123.9 us)
Sparse Core Ops, SparseCore 0:
  11.3 56.7 all-gather.4
  71.2 50.7 all-gather.2
  284.0 85.1 reduce-scatter.6
  373.3 87.2 reduce-scatter.4
  463.0 62.8 reduce-scatter.10
  528.4 69.6 reduce-scatter.8
  601.3 153.5 all-reduce.1
where the time goes:
time: 765 us; the launch traced here: 764 us
  waiting for transfers between devices  530 us (69%)
  blocking collectives  97.9 us (13%)
  matrix products  50.9 us (7%)
  local copies, waits for them, and re-layouts  33.1 us (4%)
  starting transfers between devices  24.3 us (3%)
  between operations  14.8 us (2%)
  other arithmetic  12.8 us (2%)
    ppermute x8, waiting for transfers between devices, partner_2(): return lax.ppermute(value, axis, pairs)  105 us
    psum x1, waiting for transfers between devices, per_device(): second_sum, first_sum = lax.psum((second_part, first_part), 'tp')  80 us
    psum x1, blocking collectives, per_device(): second_sum, first_sum = lax.psum((second_part, first_part), 'tp')  73.2 us
    reduce_scatter x1, waiting for transfers between devices, per_device(): lax.psum_scatter(jnp.stack(self_terms), 'seq', scatter_dimension=2, tiled...  70.6 us
    reduce_scatter x1, waiting for transfers between devices, per_device(): lax.psum_scatter(down_term, 'tp', scatter_dimension=1, tiled=True)  70.1 us
    reduce_scatter x1, waiting for transfers between devices, per_device(): lax.psum_scatter(jnp.stack(cross_terms), 'seq', scatter_dimension=2, tile...  62.4 us
    reduce_scatter x1, waiting for transfers between devices, per_device(): lax.psum_scatter(spread, 'tp', scatter_dimension=1, tiled=True)  59.9 us
    all_gather x1, waiting for transfers between devices, per_device(): lax.all_gather(hidden_in, 'tp', axis=1, tiled=True)  49.2 us
  transfers between devices with their start and end apart: 17, of which 16 were waited for; matrix products, arithmetic and copies ran while one was open for 6% of the time, Pallas kernels for 0%

commit v1 on v0

--- a/solution.py
+++ b/solution.py
@@ -65,7 +65,9 @@
         tokens.astype(jnp.float32) + mixed_tokens.reshape(seq_len, width_local).astype(jnp.float32)
     ).astype(jnp.bfloat16)
     hidden_all, cotangent_all = (
-        lax.all_gather(hidden_in, "tp", axis=1, tiled=True),
+        jnp.concatenate(
+            lax.all_to_all(jnp.stack([hidden_in] * lax.axis_size("tp")), "tp", 0, 0), axis=1
+        ),
         lax.all_gather(cotangent, "tp", axis=1, tiled=True),
     )
     flat_pairs = block_pairs.reshape(-1)

time: 765 us -> 731 us (0.956)
  waiting for transfers between devices: 530 us -> 481 us
  starting transfers between devices: 24.3 us -> 41 us
    all_gather x1 -> x0, waiting for transfers between devices: 49.2 us -> none  [per_device(): lax.all_gather(hidden_in, 'tp', axis=1, tiled=True)]
    all_to_all x0 -> x1, waiting for transfers between devices: none -> 31.1 us  [per_device(): lax.all_to_all(jnp.stack([hidden_in] * lax.axis_size('tp')), 'tp', 0, 0)]
    all_gather x1, waiting for transfers between devices: 25.5 us -> 0.01 us  [per_device(): lax.all_gather(cotangent, 'tp', axis=1, tiled=True)]
    all_to_all x0 -> x1, starting transfers between devices: none -> 9.82 us  [per_device(): lax.all_to_all(jnp.stack([hidden_in] * lax.axis_size('tp')), 'tp', 0, 0)]
  transfers between devices with their start and end apart: 17 -> 17, of which waited for: 16 -> 15; matrix products, arithmetic and copies ran while one was open for 6% -> 6% of each run, Pallas kernels for 0% -> 0%
where the time goes in v1:
time: 731 us; the launch traced here: 730 us
  waiting for transfers between devices  481 us (66%)
  blocking collectives  98.2 us (13%)
  matrix products  50 us (7%)
  starting transfers between devices  41 us (6%)
  local copies, waits for them, and re-layouts  31.6 us (4%)
  between operations  14.8 us (2%)
  other arithmetic  13.7 us (2%)
    ppermute x8, waiting for transfers between devices, partner_2(): return lax.ppermute(value, axis, pairs)  101 us
    psum x1, waiting for transfers between devices, per_device(): second_sum, first_sum = lax.psum((second_part, first_part), 'tp')  79.7 us
    psum x1, blocking collectives, per_device(): second_sum, first_sum = lax.psum((second_part, first_part), 'tp')  73.5 us
    reduce_scatter x1, waiting for transfers between devices, per_device(): lax.psum_scatter(jnp.stack(self_terms), 'seq', scatter_dimension=2, tiled...  70.6 us
    reduce_scatter x1, waiting for transfers between devices, per_device(): lax.psum_scatter(down_term, 'tp', scatter_dimension=1, tiled=True)  70.3 us
    reduce_scatter x1, waiting for transfers between devices, per_device(): lax.psum_scatter(jnp.stack(cross_terms), 'seq', scatter_dimension=2, tile...  62.1 us
    reduce_scatter x1, waiting for transfers between devices, per_device(): lax.psum_scatter(spread, 'tp', scatter_dimension=1, tiled=True)  58.8 us
    all_to_all x1, waiting for transfers between devices, per_device(): lax.all_to_all(jnp.stack([hidden_in] * lax.axis_size('tp')), 'tp', 0, 0)  31.1 us
  transfers between devices with their start and end apart: 17, of which 15 were waited for; matrix products, arithmetic and copies ran while one was open for 6% of the time, Pallas kernels for 0%

profile of v1, /device:TPU:1, one launch (start us, length us, event | category | flops | bytes accessed | tf_op | source)
XLA Modules:
  0.0 730.2 jit_solution(15245738370927005198)
XLA Ops:
  13.0 10.0 %all-to-all-start = ((bf16[16,2,2048]{2,1,0:T(2,128)(2,1)}), bf16[16,2,2048]{2,1,0:T(2,128)(2,1)S(1)}, u32[]{:S(2)}, u32[]{:S(2)}) async-start(bf16[16,2,2048]{2,1,0:T(2,128)(2,1)} %reshape.153), calls=%async_computation | async-start | bytes 262144 | tf_op jit(solution)/shard_map/all_to_all | solution.py:55
  23.3 7.3 %all-to-all-done = bf16[16,2,2048]{2,1,0:T(2,128)(2,1)S(1)} async-done(((bf16[16,2,2048]{2,1,0:T(2,128)(2,1)}), bf16[16,2,2048]{2,1,0:T(2,128)(2,1)S(1)}, u32[]{:S(2)}, u32[]{:S(2)}) %all-to-all-start) | async-done | bytes 131104 | tf_op jit(solution)/shard_map/all_to_all | solution.py:55
  31.0 10.6 %all_to_all.47 = bf16[16,32,128]{2,1,0:T(8,128)(2,1)S(1)} all-to-all(bf16[16,32,128]{2,1,0:T(8,128)(2,1)S(1)} %copy.133), channel_id=1, replica_groups=mesh['seq'=16,'tp'=16] {'seq'}, dimensions={0} | all-to-all | bytes 262144 | tf_op jit(solution)/shard_map/all_to_all | solution.py:61
  43.5 9.8 %all-to-all-start.2 = ((bf16[16,512,128]{2,1,0:T(8,128)(2,1)}), bf16[16,512,128]{2,1,0:T(8,128)(2,1)S(1)}, u32[]{:S(2)}, u32[]{:S(2)}) async-start(bf16[16,512,128]{2,1,0:T(8,128)(2,1)} %stack.30), calls=%async_computation.2 | async-start | bytes 4194304 | tf_op jit(solution)/shard_map/all_to_all | solution.py:69
  53.6 31.1 %all-to-all-done.2 = bf16[16,512,128]{2,1,0:T(8,128)(2,1)S(1)} async-done(((bf16[16,512,128]{2,1,0:T(8,128)(2,1)}), bf16[16,512,128]{2,1,0:T(8,128)(2,1)S(1)}, u32[]{:S(2)}, u32[]{:S(2)}) %all-to-all-start.2) | async-done | bytes 2097184 | tf_op jit(solution)/shard_map/all_to_all | solution.py:69
  103.4 12.4 %collective-permute-done.1 = bf16[512,4,128]{2,0,1:T(8,128)(2,1)S(1)} collective-permute-done((bf16[512,4,128]{2,0,1:T(8,128)(2,1)S(1)}, bf16[512,4,128]{2,0,1:T(8,128)(2,1)S(1)}, u32[]{:S(2)}, u32[]{:S(2)}) %collective-permute-start.1) | collective-permute-done | bytes 524320 | tf_op jit(solution)/shard_map/ppermute | solution.py:11
  116.1 3.9 collective-permute-start.2
  120.2 11.1 %collective-permute-done.2 = bf16[512,4,128]{2,0,1:T(8,128)(2,1)S(1)} collective-permute-done((bf16[512,4,128]{2,0,1:T(8,128)(2,1)S(1)}, bf16[512,4,128]{2,0,1:T(8,128)(2,1)S(1)}, u32[]{:S(2)}, u32[]{:S(2)}) %collective-permute-start.2) | collective-permute-done | bytes 524320 | tf_op jit(solution)/shard_map/ppermute | solution.py:11
  134.7 10.9 %collective-permute-done.3 = bf16[512,4,128]{2,0,1:T(8,128)(2,1)S(1)} collective-permute-done((bf16[512,4,128]{2,0,1:T(8,128)(2,1)S(1)}, bf16[512,4,128]{2,0,1:T(8,128)(2,1)S(1)}, u32[]{:S(2)}, u32[]{:S(2)}) %collective-permute-start.3) | collective-permute-done | bytes 524320 | tf_op jit(solution)/shard_map/ppermute | solution.py:11
  149.9 21.5 %collective-permute-done.4 = f32[512,4,128]{2,0,1:T(8,128)S(1)} collective-permute-done((f32[512,4,128]{2,0,1:T(8,128)S(1)}, f32[512,4,128]{2,0,1:T(8,128)S(1)}, u32[]{:S(2)}, u32[]{:S(2)}) %collective-permute-start.4) | collective-permute-done | bytes 1048608 | tf_op jit(solution)/shard_map/ppermute | solution.py:11
  174.5 20.8 %collective-permute-done.5 = f32[512,4,128]{2,0,1:T(8,128)S(1)} collective-permute-done((f32[512,4,128]{2,0,1:T(8,128)S(1)}, f32[512,4,128]{2,0,1:T(8,128)S(1)}, u32[]{:S(2)}, u32[]{:S(2)}) %collective-permute-start.5) | collective-permute-done | bytes 1048608 | tf_op jit(solution)/shard_map/ppermute | solution.py:11
  196.0 20.6 %collective-permute-done.6 = f32[512,4,128]{2,0,1:T(8,128)S(1)} collective-permute-done((f32[512,4,128]{2,0,1:T(8,128)S(1)}, f32[512,4,128]{2,0,1:T(8,128)S(1)}, u32[]{:S(2)}, u32[]{:S(2)}) %collective-permute-start.6) | collective-permute-done | bytes 1048608 | tf_op jit(solution)/shard_map/ppermute | solution.py:11
  217.2 5.0 collective-permute-start.7
  237.8 7.2 convolution_bitcast_fusion
  245.0 5.4 copy.185
  253.0 4.1 fusion.1
  257.1 4.0 copy.203
  276.5 58.8 %reduce-scatter.7.cloned.1.call-done = f32[512,128]{0,1:T(8,128)} async-done(((f32[512,2048]{0,1:T(8,128)}), f32[512,128]{0,1:T(8,128)}) %reduce-scatter.7.cloned.1.call-update) | async-done | bytes 262160 | tf_op jit(solution)/shard_map/reduce_scatter | solution.py:128
  338.0 14.1 %all_to_all.48 = bf16[16,2,2048]{2,1,0:T(2,128)(2,1)S(1)} all-to-all(bf16[16,2,2048]{2,1,0:T(2,128)(2,1)S(1)} %reshape.155), channel_id=1, replica_groups=mesh['seq'=16,'tp'=16] {'seq'}, dimensions={0} | all-to-all | bytes 262144 | tf_op jit(solution)/shard_map/all_to_all | solution.py:134
  356.7 70.3 %reduce-scatter.5.cloned.1.call-done = f32[512,128]{1,0:T(8,128)} async-done(((f32[512,2048]{1,0:T(8,128)}), f32[512,128]{1,0:T(8,128)}) %reduce-scatter.5.cloned.1.call-update) | async-done | bytes 262160 | tf_op jit(solution)/shard_map/reduce_scatter | solution.py:101
  429.9 62.1 %reduce-scatter.11.cloned.1.call-done = f32[6,4,8,128]{3,2,1,0:T(8,128)} async-done(((f32[6,4,128,128]{3,2,1,0:T(8,128)}), f32[6,4,8,128]{3,2,1,0:T(8,128)}) %reduce-scatter.11.cloned.1.call-update) | async-done | bytes 98320 | tf_op jit(solution)/shard_map/reduce_scatter | solution.py:132
  493.6 70.6 %reduce-scatter.9.cloned.1.call-done = f32[6,4,8,128]{3,2,1,0:T(8,128)} async-done(((f32[6,4,128,128]{3,2,1,0:T(8,128)}), f32[6,4,8,128]{3,2,1,0:T(8,128)}) %reduce-scatter.9.cloned.1.call-update) | async-done | bytes 98320 | tf_op jit(solution)/shard_map/reduce_scatter | solution.py:131
  565.9 73.5 %psum.15 = f32[32,16,16]{2,1,0:T(8,128)S(1)} all-reduce(f32[32,16,16]{2,1,0:T(8,128)S(1)} %fusion.97), channel_id=1, replica_groups=mesh['seq'=16,'tp'=16] {'tp'}, use_global_device_ids=true, to_apply=%region_3.5 | all-reduce | flops 8192 | bytes 65536 | tf_op jit(solution)/shard_map/psum | solution.py:149
  641.3 79.7 %all-reduce.2.cloned.1.call-done = f32[1,512,512]{2,1,0:T(8,128)} async-done(((f32[1,512,512]{2,1,0:T(8,128)}), f32[1,512,512]{2,1,0:T(8,128)}) %all-reduce.2.cloned.1.call-update) | async-done | bytes 1048592 | tf_op jit(solution)/shard_map/psum | solution.py:149
  (194 shorter events, 90.6 us)
Async XLA Ops:
  7.2 79.1 %all-gather.2.cloned.1.call-start = ((), (), s32[]{:S(2)}) async-start(), calls=%async_computation.10 | async-start | bytes 2228224 | tf_op jit(solution)/shard_map/all_gather | solution.py:71
  10.2 31.4 %copy-start.30 = (bf16[512,128]{1,0:T(8,128)(2,1)S(1)}, bf16[512,128]{1,0:T(8,128)(2,1)}, u32[]{:S(2)}) copy-start(bf16[512,128]{1,0:T(8,128)(2,1)} %param.11) | copy-start | bytes 393220
  13.0 17.6 %all-to-all-start = ((bf16[16,2,2048]{2,1,0:T(2,128)(2,1)}), bf16[16,2,2048]{2,1,0:T(2,128)(2,1)S(1)}, u32[]{:S(2)}, u32[]{:S(2)}) async-start(bf16[16,2,2048]{2,1,0:T(2,128)(2,1)} %reshape.153), calls=%async_computation | async-start | bytes 262144 | tf_op jit(solution)/shard_map/all_to_all | solution.py:55
  43.5 41.2 %all-to-all-start.2 = ((bf16[16,512,128]{2,1,0:T(8,128)(2,1)}), bf16[16,512,128]{2,1,0:T(8,128)(2,1)S(1)}, u32[]{:S(2)}, u32[]{:S(2)}) async-start(bf16[16,512,128]{2,1,0:T(8,128)(2,1)} %stack.30), calls=%async_computation.2 | async-start | bytes 4194304 | tf_op jit(solution)/shard_map/all_to_all | solution.py:69
  53.3 282.0 %reduce-scatter.7.cloned.1.call-start = ((), (), s32[]{:S(2)}) async-start(), calls=%async_computation.11 | async-start | bytes 4456448 | tf_op jit(solution)/shard_map/reduce_scatter | solution.py:128
  99.6 2.2 collective-permute-start
  102.6 13.1 %collective-permute-start.1 = (bf16[512,4,128]{2,0,1:T(8,128)(2,1)S(1)}, bf16[512,4,128]{2,0,1:T(8,128)(2,1)S(1)}, u32[]{:S(2)}, u32[]{:S(2)}) collective-permute-start(bf16[512,4,128]{2,0,1:T(8,128)(2,1)S(1)} %fusion.27), channel_id=1, source_target_pairs={{0,2},{1,3},{2,0},{3,1},{4,6},{5,7},{6,4},{7,5},{8,10},{9,11},{10,... | collective-permute-start | bytes 1572872 | tf_op jit(solution)/shard_map/ppermute | solution.py:11
  116.1 15.2 %collective-permute-start.2 = (bf16[512,4,128]{2,0,1:T(8,128)(2,1)S(1)}, bf16[512,4,128]{2,0,1:T(8,128)(2,1)S(1)}, u32[]{:S(2)}, u32[]{:S(2)}) collective-permute-start(bf16[512,4,128]{2,0,1:T(8,128)(2,1)S(1)} %fusion.26), channel_id=1, source_target_pairs={{0,4},{1,5},{2,6},{3,7},{4,0},{5,1},{6,2},{7,3},{8,12},{9,13},{10,... | collective-permute-start | bytes 1572872 | tf_op jit(solution)/shard_map/ppermute | solution.py:11
  132.1 13.5 %collective-permute-start.3 = (bf16[512,4,128]{2,0,1:T(8,128)(2,1)S(1)}, bf16[512,4,128]{2,0,1:T(8,128)(2,1)S(1)}, u32[]{:S(2)}, u32[]{:S(2)}) collective-permute-start(bf16[512,4,128]{2,0,1:T(8,128)(2,1)S(1)} %fusion.25), channel_id=1, source_target_pairs={{0,8},{1,9},{2,10},{3,11},{4,12},{5,13},{6,14},{7,15},{8,0},{9,1},... | collective-permute-start | bytes 1572872 | tf_op jit(solution)/shard_map/ppermute | solution.py:11
  147.2 24.5 %copy-start.4 = (bf16[512,4,128]{2,0,1:T(8,128)(2,1)}, bf16[512,4,128]{2,0,1:T(8,128)(2,1)S(1)}, u32[]{:S(2)}) copy-start(bf16[512,4,128]{2,0,1:T(8,128)(2,1)S(1)} %fusion.52) | copy-start | bytes 1572868
  147.5 23.9 %collective-permute-start.4 = (f32[512,4,128]{2,0,1:T(8,128)S(1)}, f32[512,4,128]{2,0,1:T(8,128)S(1)}, u32[]{:S(2)}, u32[]{:S(2)}) collective-permute-start(f32[512,4,128]{2,0,1:T(8,128)S(1)} %convolution_bitcast_fusion.12), channel_id=1, source_target_pairs={{0,8},{1,9},{2,10},{3,11},{4,12},{5,13},{6,14},{7,15},{8,0},{9,1},... | collective-permute-start | bytes 3145736 | tf_op jit(solution)/shard_map/ppermute | solution.py:11
  172.1 23.2 %collective-permute-start.5 = (f32[512,4,128]{2,0,1:T(8,128)S(1)}, f32[512,4,128]{2,0,1:T(8,128)S(1)}, u32[]{:S(2)}, u32[]{:S(2)}) collective-permute-start(f32[512,4,128]{2,0,1:T(8,128)S(1)} %convolution_bitcast_fusion.10), channel_id=1, source_target_pairs={{0,4},{1,5},{2,6},{3,7},{4,0},{5,1},{6,2},{7,3},{8,12},{9,13},{10,... | collective-permute-start | bytes 3145736 | tf_op jit(solution)/shard_map/ppermute | solution.py:11
  195.9 20.7 %collective-permute-start.6 = (f32[512,4,128]{2,0,1:T(8,128)S(1)}, f32[512,4,128]{2,0,1:T(8,128)S(1)}, u32[]{:S(2)}, u32[]{:S(2)}) collective-permute-start(f32[512,4,128]{2,0,1:T(8,128)S(1)} %convolution_bitcast_fusion.8), channel_id=1, source_target_pairs={{0,2},{1,3},{2,0},{3,1},{4,6},{5,7},{6,4},{7,5},{8,10},{9,11},{10,... | collective-permute-start | bytes 3145736 | tf_op jit(solution)/shard_map/ppermute | solution.py:11
  217.2 7.3 %collective-permute-start.7 = (f32[512,4,128]{2,0,1:T(8,128)S(1)}, f32[512,4,128]{2,0,1:T(8,128)S(1)}, u32[]{:S(2)}, u32[]{:S(2)}) collective-permute-start(f32[512,4,128]{2,0,1:T(8,128)S(1)} %convolution_bitcast_fusion.6), channel_id=1, source_target_pairs={{0,1},{1,0},{2,3},{3,2},{4,5},{5,4},{6,7},{7,6},{8,9},{9,8},{10,11... | collective-permute-start | bytes 3145736 | tf_op jit(solution)/shard_map/ppermute | solution.py:11
  250.4 176.6 %reduce-scatter.5.cloned.1.call-start = ((), (), s32[]{:S(2)}) async-start(), calls=%async_computation.9 | async-start | bytes 4456448 | tf_op jit(solution)/shard_map/reduce_scatter | solution.py:101
  261.1 230.9 %reduce-scatter.11.cloned.1.call-start = ((), (), s32[]{:S(2)}) async-start(), calls=%async_computation.14 | async-start | bytes 1671168 | tf_op jit(solution)/shard_map/reduce_scatter | solution.py:132
  268.9 295.3 %reduce-scatter.9.cloned.1.call-start = ((), (), s32[]{:S(2)}) async-start(), calls=%async_computation.13 | async-start | bytes 1671168 | tf_op jit(solution)/shard_map/reduce_scatter | solution.py:131
  275.4 59.9 %copy-start.27 = (bf16[512,128]{0,1:T(8,128)(2,1)S(1)}, bf16[512,128]{0,1:T(8,128)(2,1)}, u32[]{:S(2)}) copy-start(bf16[512,128]{0,1:T(8,128)(2,1)} %copy.140) | copy-start | bytes 393220
  336.3 90.7 %copy-start.35 = (bf16[512,128]{1,0:T(8,128)(2,1)S(1)}, bf16[512,128]{1,0:T(8,128)(2,1)}, u32[]{:S(2)}) copy-start(bf16[512,128]{1,0:T(8,128)(2,1)} %copy-done.34) | copy-start | bytes 393220
  336.5 92.1 %copy-start.31 = (bf16[512,128]{1,0:T(8,128)(2,1)S(1)}, bf16[512,128]{1,0:T(8,128)(2,1)}, u32[]{:S(2)}) copy-start(bf16[512,128]{1,0:T(8,128)(2,1)} %param.11) | copy-start | bytes 393220
  353.2 75.5 %all-to-all-start.4 = ((bf16[16,32,128]{2,1,0:T(8,128)(2,1)}), bf16[16,32,128]{2,1,0:T(8,128)(2,1)S(1)}, u32[]{:S(2)}, u32[]{:S(2)}) async-start(bf16[16,32,128]{2,1,0:T(8,128)(2,1)} %copy.148), calls=%async_computation.6 | async-start | bytes 262144 | tf_op jit(solution)/shard_map/all_to_all | solution.py:144
  356.7 209.0 %copy-start.33 = (bf16[1,512,128]{2,1,0:T(8,128)(2,1)S(1)}, bf16[1,512,128]{2,1,0:T(8,128)(2,1)}, u32[]{:S(2)}) copy-start(bf16[1,512,128]{2,1,0:T(8,128)(2,1)} %copy-done.32) | copy-start | bytes 393220
  356.7 364.3 %all-reduce.2.cloned.1.call-start = ((), (), s32[]{:S(2)}) async-start(), calls=%async_computation.12 | async-start | bytes 2097152 | tf_op jit(solution)/shard_map/psum | solution.py:149
  429.9 210.4 %copy-start.39 = (f32[512,128]{0,1:T(8,128)S(1)}, f32[512,128]{0,1:T(8,128)}, u32[]{:S(2)}) copy-start(f32[512,128]{0,1:T(8,128)} %reduce-scatter.7.cloned.1.call-done) | copy-start | bytes 786436
  (37 other events, 170.0 us)
Sparse Core Ops, SparseCore 0:
  11.3 68.7 all-gather.1
  250.5 84.8 reduce-scatter.6
  339.6 87.3 reduce-scatter.4
  429.4 62.5 reduce-scatter.10
  494.4 69.7 reduce-scatter.8
  567.2 153.7 all-reduce.1
